TPU v7x, 32 devices: a whole 2x2x4 slice. The times are simulated.
32 devices in a mesh: cuts: 2 (over y), group: 16 (over z, x, core).
Axes of the slice: x: 2, y: 2, z: 4, core: 2. Of those that a mesh axis runs over, the one named last changes fastest.
Arguments:
- stem_blocks: bfloat16 [2, 64, 1024, 512], P('cuts', None, 'group'), may hold values from -6 to 6
- cap_tensor: bfloat16 [2, 2, 256, 256], P('cuts'), may hold values from -0.1875 to 0.1875
- slot_rows: int32 [64, 1024], P('group'), may hold values from 0 to 1023
- counts: int32 [64], P('group'), may hold values from 128 to 1024, as said below
Outputs:
- amplitudes: bfloat16 [1024, 64, 512], P('cuts', 'group')
Inputs may be any that keep to these rules, and one draw needn't show every extreme that they name: `counts`: some group has exactly 1024 live slots in every draw.
All inputs are finite; a program needn't handle non-finite values.
Results may differ from a plain program's by a relative error of at most 0.0052.
Values may be sent and summed in bfloat16 or wider, within the bound.
No kernel may reach another device: no remote copies, remote signals or barrier semaphores. Data moves between devices by JAX's collectives and lax.ppermute only.
A program may use at most 64 MiB of HBM per device.

v0:
```python
import jax
import jax.numpy as jnp
from jax import lax
from jax.sharding import PartitionSpec as P


def build_matrix(cap_pair):
    real_part = cap_pair[0]
    imag_part = cap_pair[1]
    upper = jnp.concatenate([real_part, imag_part], axis=1)
    lower = jnp.concatenate([-imag_part, real_part], axis=1)
    return jnp.concatenate([upper, lower], axis=0)


def local(stem_blocks, cap_tensor, slot_rows, counts):
    owned_rows = lax.all_to_all(stem_blocks[0], "group", split_axis=0, concat_axis=1, tiled=True)
    matrix = build_matrix(cap_tensor[0])
    slot_total = slot_rows.shape[1]
    share = slot_total // lax.axis_size("cuts")
    positions = jnp.arange(slot_total, dtype=jnp.int32)
    live_mask = positions[None, :] < counts[:, None]
    picked = jnp.take_along_axis(owned_rows, slot_rows[:, :, None], axis=1)
    product = jnp.einsum("gcr,rs->cgs", picked, matrix, preferred_element_type=jnp.float32)
    whole_sum = lax.psum(
        jnp.where(jnp.transpose(live_mask)[:, :, None], product, jnp.float32(0.0)).astype(
            jnp.bfloat16
        ),
        "cuts",
    ).astype(jnp.float32)
    summed = lax.dynamic_slice_in_dim(whole_sum, lax.axis_index("cuts") * share, share, 0)
    return summed.astype(jnp.bfloat16)


def solution(mesh):
    in_specs = (
        P("cuts", None, "group", None),
        P("cuts", None, None, None),
        P("group", None),
        P("group"),
    )
    out_specs = P("cuts", "group", None)
    return jax.shard_map(local, mesh=mesh, in_specs=in_specs, out_specs=out_specs, check_vma=False)
```

profile of v0, /device:TPU:0, one launch (start us, length us, event | category | flops | bytes accessed | tf_op | source)
XLA Modules:
  0.0 309.5 jit_solution(17406738748968861879)
XLA Ops:
  6.5 0.0 copy-start.1
  6.5 0.0 copy-start
  6.5 0.0 copy-start.2
  6.5 7.5 %all-to-all-start = ((bf16[64,64,512]{2,1,0:T(8,128)(2,1)}), bf16[64,64,512]{2,1,0:T(8,128)(2,1)}, u32[]{:S(2)}, u32[]{:S(2)}) async-start(bf16[64,64,512]{2,1,0:T(8,128)(2,1)} %bitcast.29), calls=%async_computation | async-start | bytes 8388608 | tf_op jit(solution)/shard_map/all_to_all | solution.py:16
  14.1 0.0 all-reduce.2.cloned.1.call-start
  14.1 0.0 copy-done.1
  14.2 0.0 copy-done
  14.2 0.1 copy.9
  14.3 0.1 copy.10
  14.4 0.0 copy-done.2
  14.4 0.1 iota_compare_fusion
  14.6 77.2 %all-to-all-done = bf16[64,64,512]{2,1,0:T(8,128)(2,1)} async-done(((bf16[64,64,512]{2,1,0:T(8,128)(2,1)}), bf16[64,64,512]{2,1,0:T(8,128)(2,1)}, u32[]{:S(2)}, u32[]{:S(2)}) %all-to-all-start) | async-done | bytes 4194336 | tf_op jit(solution)/shard_map/all_to_all | solution.py:16
  91.8 4.6 %copy.7 = bf16[16,4,64,512]{3,2,0,1:T(8,128)(2,1)} copy(bf16[16,4,64,512]{3,2,1,0:T(8,128)(2,1)} %bitcast.4) | data formatting | bytes 8388608 | tf_op jit(solution)/shard_map/all_to_all | solution.py:16
  96.4 72.6 %gather_fusion = bf16[4096,512]{1,0:T(8,128)(2,1)} fusion(bf16[4,1024,512]{2,1,0:T(8,128)(2,1)} %bitcast.26, s32[4096]{0:T(1024)S(1)} %bitcast.27), kind=kCustom, calls=%fused_computation | custom fusion | bytes 8421376 | tf_op jit(solution)/shard_map/jit(take_along_axis)/gather | solution.py:22
  169.0 5.8 %fusion = bf16[1024,4,512]{0,2,1:T(8,128)(2,1)} fusion(pred[1024,4]{0,1:T(4,128)(4,1)S(1)} %iota_compare_fusion, bf16[4,1024,512]{2,1,0:T(8,128)(2,1)} %bitcast.28, pred[4,1024]{1,0:T(4,128)(4,1)S(1)} %compare_and_fusion, bf16[256,256]{0,1:T(8,128)(2,1)S(1)} %bitcast.31, bf16[256,256]{0,1:T(8,128)(2,1)S(1)} %bitcast_negate_fusion, ...), kind=kOutput, calls=%fused_computation.2 | convolution fusion | flops 2155872256 | bytes 8790016 | tf_op jit(solution)/shard_map/gcr,rs->cgs/dot_general | solution.py:23
  174.8 0.0 all-reduce.2.cloned.1.call-update
  174.9 123.0 %all-reduce.2.cloned.1.call-done = bf16[1024,4,512]{0,2,1:T(8,128)(2,1)} async-done(((bf16[1024,4,512]{0,2,1:T(8,128)(2,1)}), bf16[1024,4,512]{0,2,1:T(8,128)(2,1)}) %all-reduce.2.cloned.1.call-update) | async-done | bytes 4194320 | tf_op jit(solution)/shard_map/psum | solution.py:24
  297.9 1.7 convert_convert_fusion
  299.6 3.1 copy.8
  (5 shorter events, 0.1 us)
Async XLA Ops:
  6.5 7.6 %copy-start.1 = (s32[4,1024]{1,0:T(4,128)S(1)}, s32[4,1024]{1,0:T(4,128)}, u32[]{:S(2)}) copy-start(s32[4,1024]{1,0:T(4,128)} %param.6) | copy-start | bytes 49156
  6.5 7.6 %copy-start = (bf16[1,2,256,256]{3,2,1,0:T(8,128)(2,1)S(1)}, bf16[1,2,256,256]{3,2,1,0:T(8,128)(2,1)}, u32[]{:S(2)}) copy-start(bf16[1,2,256,256]{3,2,1,0:T(8,128)(2,1)} %param.5) | copy-start | bytes 786436
  6.5 7.9 %copy-start.2 = (s32[4]{0:T(128)S(1)}, s32[4]{0:T(128)}, u32[]{:S(2)}) copy-start(s32[4]{0:T(128)} %param.7) | copy-start | bytes 52
  6.5 85.2 %all-to-all-start = ((bf16[64,64,512]{2,1,0:T(8,128)(2,1)}), bf16[64,64,512]{2,1,0:T(8,128)(2,1)}, u32[]{:S(2)}, u32[]{:S(2)}) async-start(bf16[64,64,512]{2,1,0:T(8,128)(2,1)} %bitcast.29), calls=%async_computation | async-start | bytes 8388608 | tf_op jit(solution)/shard_map/all_to_all | solution.py:16
  14.1 283.8 %all-reduce.2.cloned.1.call-start = ((), (), s32[]{:S(2)}) async-start(), calls=%async_computation.1 | async-start | bytes 8388608 | tf_op jit(solution)/shard_map/psum | solution.py:24
Sparse Core Ops, SparseCore 0:
  175.0 122.8 all-reduce.1
where the time goes:
time: 311 us; the launch traced here: 310 us
  waiting for transfers between devices  200 us (64%)
  local copies, waits for them, and re-layouts  80.5 us (26%)
  between operations  13.5 us (4%)
  starting transfers between devices  7.58 us (2%)
  matrix products  5.84 us (2%)
    psum x1, waiting for transfers between devices, local(): lax.psum(jnp.where(jnp.transpose(live_mask)[:, :, None], product, jnp.flo...  123 us
    all_to_all x1, waiting for transfers between devices, local(): lax.all_to_all(stem_blocks[0], 'group', split_axis=0, concat_axis=1, tile...  77.2 us
    gather x1, local copies, waits for them, and re-layouts, local(): picked = jnp.take_along_axis(owned_rows, slot_rows[:, :, None], axis=1)  72.6 us
    all_to_all x1, starting transfers between devices, local(): lax.all_to_all(stem_blocks[0], 'group', split_axis=0, concat_axis=1, tile...  7.54 us
  transfers between devices with their start and end apart: 2, of which 2 were waited for; matrix products, arithmetic and copies ran while one was open for 0% of the time, Pallas kernels for 0%

commit v1 on v0

--- a/solution.py
+++ b/solution.py
@@ -13,7 +13,12 @@
 
 
 def local(stem_blocks, cap_tensor, slot_rows, counts):
-    owned_rows = lax.all_to_all(stem_blocks[0], "group", split_axis=0, concat_axis=1, tiled=True)
+    owned_rows = jnp.concatenate(
+        lax.all_to_all(
+            jnp.stack(jnp.split(stem_blocks[0], lax.axis_size("group"), axis=0)), "group", 0, 0
+        ),
+        axis=1,
+    )
     matrix = build_matrix(cap_tensor[0])
     slot_total = slot_rows.shape[1]
     share = slot_total // lax.axis_size("cuts")

time: 311 us -> 338 us (1.087)
  local copies, waits for them, and re-layouts: 80.5 us -> 107 us
    unnamed x9 -> x24, local copies, waits for them, and re-layouts: 0.21 us -> 25.3 us
    reshape x0 -> x1, local copies, waits for them, and re-layouts: none -> 4.66 us  [local(): jnp.concatenate(lax.all_to_all(jnp.stack(jnp.split(stem_blocks[0], lax.ax...]
    all_to_all x1 -> x0, local copies, waits for them, and re-layouts: 4.63 us -> none  [local(): lax.all_to_all(stem_blocks[0], 'group', split_axis=0, concat_axis=1, tile...]
where the time goes in v1:
time: 338 us; the launch traced here: 336 us
  waiting for transfers between devices  200 us (59%)
  local copies, waits for them, and re-layouts  107 us (32%)
  between operations  13.5 us (4%)
  starting transfers between devices  7.58 us (2%)
  matrix products  5.85 us (2%)
    psum x1, waiting for transfers between devices, local(): lax.psum(jnp.where(jnp.transpose(live_mask)[:, :, None], product, jnp.flo...  123 us
    all_to_all x1, waiting for transfers between devices, local(): lax.all_to_all(jnp.stack(jnp.split(stem_blocks[0], lax.axis_size('group')...  77.2 us
    gather x1, local copies, waits for them, and re-layouts, local(): picked = jnp.take_along_axis(owned_rows, slot_rows[:, :, None], axis=1)  72.5 us
    unnamed x24, local copies, waits for them, and re-layouts  25.3 us
    all_to_all x1, starting transfers between devices, local(): lax.all_to_all(jnp.stack(jnp.split(stem_blocks[0], lax.axis_size('group')...  7.54 us
  transfers between devices with their start and end apart: 2, of which 2 were waited for; matrix products, arithmetic and copies ran while one was open for 0% of the time, Pallas kernels for 0%

profile of v1, /device:TPU:0, one launch (start us, length us, event | category | flops | bytes accessed | tf_op | source)
XLA Modules:
  0.0 336.3 jit_solution(17806805747414089276)
XLA Ops:
  6.5 1.7 slice_dynamic-update-slice_fusion.15
  8.2 1.7 slice_dynamic-update-slice_fusion.14
  9.9 1.7 slice_dynamic-update-slice_fusion.13
  11.6 1.7 slice_dynamic-update-slice_fusion.12
  13.3 1.7 slice_dynamic-update-slice_fusion.11
  15.0 1.7 slice_dynamic-update-slice_fusion.10
  16.6 1.7 slice_dynamic-update-slice_fusion.9
  18.3 1.7 slice_dynamic-update-slice_fusion.8
  20.0 1.7 slice_dynamic-update-slice_fusion.7
  21.6 1.7 slice_dynamic-update-slice_fusion.6
  23.3 1.7 slice_dynamic-update-slice_fusion.5
  25.0 1.7 slice_dynamic-update-slice_fusion.4
  26.6 1.7 slice_dynamic-update-slice_fusion.3
  28.3 1.7 slice_dynamic-update-slice_fusion.2
  30.0 1.7 slice_dynamic-update-slice_fusion.1
  31.6 1.7 slice_dynamic-update-slice_fusion
  33.4 7.5 %all-to-all-start = ((bf16[16,4,64,512]{3,2,1,0:T(8,128)(2,1)}), bf16[16,4,64,512]{3,2,1,0:T(8,128)(2,1)}, u32[]{:S(2)}, u32[]{:S(2)}) async-start(bf16[16,4,64,512]{3,2,1,0:T(8,128)(2,1)} %slice_dynamic-update-slice_fusion), calls=%async_computation | async-start | bytes 8388608 | tf_op jit(solution)/shard_map/all_to_all | solution.py:17
  40.9 0.0 all-reduce.2.cloned.1.call-start
  41.0 0.0 copy-done.1
  41.0 0.0 copy-done
  41.0 0.1 copy.9
  41.1 0.1 copy.10
  41.3 0.0 copy-done.2
  41.3 0.1 iota_compare_fusion
  41.4 77.2 %all-to-all-done = bf16[16,4,64,512]{3,2,1,0:T(8,128)(2,1)} async-done(((bf16[16,4,64,512]{3,2,1,0:T(8,128)(2,1)}), bf16[16,4,64,512]{3,2,1,0:T(8,128)(2,1)}, u32[]{:S(2)}, u32[]{:S(2)}) %all-to-all-start) | async-done | bytes 4194336 | tf_op jit(solution)/shard_map/all_to_all | solution.py:17
  118.6 4.7 %copy.7 = bf16[4,16,64,512]{3,2,1,0:T(8,128)(2,1)} copy(bf16[4,16,64,512]{3,2,0,1:T(8,128)(2,1)} %bitcast.3) | data formatting | bytes 8388608 | tf_op jit(solution)/shard_map/reshape | solution.py:16
  123.2 72.5 %gather_fusion = bf16[4096,512]{1,0:T(8,128)(2,1)} fusion(bf16[4,1024,512]{2,1,0:T(8,128)(2,1)} %bitcast.23, s32[4096]{0:T(1024)S(1)} %bitcast.24), kind=kCustom, calls=%fused_computation | custom fusion | bytes 8421376 | tf_op jit(solution)/shard_map/jit(take_along_axis)/gather | solution.py:27
  195.7 5.8 %fusion = bf16[1024,4,512]{0,2,1:T(8,128)(2,1)} fusion(pred[1024,4]{0,1:T(4,128)(4,1)S(1)} %iota_compare_fusion, bf16[4,1024,512]{2,1,0:T(8,128)(2,1)} %bitcast.25, pred[4,1024]{1,0:T(4,128)(4,1)S(1)} %compare_and_fusion, bf16[256,256]{0,1:T(8,128)(2,1)S(1)} %bitcast.27, bf16[256,256]{0,1:T(8,128)(2,1)S(1)} %bitcast_negate_fusion, ...), kind=kOutput, calls=%fused_computation.2 | convolution fusion | flops 2155872256 | bytes 8790016 | tf_op jit(solution)/shard_map/gcr,rs->cgs/dot_general | solution.py:28
  201.5 0.0 all-reduce.2.cloned.1.call-update
  201.6 123.0 %all-reduce.2.cloned.1.call-done = bf16[1024,4,512]{0,2,1:T(8,128)(2,1)} async-done(((bf16[1024,4,512]{0,2,1:T(8,128)(2,1)}), bf16[1024,4,512]{0,2,1:T(8,128)(2,1)}) %all-reduce.2.cloned.1.call-update) | async-done | bytes 4194320 | tf_op jit(solution)/shard_map/psum | solution.py:29
  324.6 1.7 convert_convert_fusion
  326.3 3.1 copy.8
  (8 shorter events, 0.1 us)
Async XLA Ops:
  33.4 7.6 %copy-start.1 = (s32[4,1024]{1,0:T(4,128)S(1)}, s32[4,1024]{1,0:T(4,128)}, u32[]{:S(2)}) copy-start(s32[4,1024]{1,0:T(4,128)} %param.6) | copy-start | bytes 49156
  33.4 7.6 %copy-start = (bf16[1,2,256,256]{3,2,1,0:T(8,128)(2,1)S(1)}, bf16[1,2,256,256]{3,2,1,0:T(8,128)(2,1)}, u32[]{:S(2)}) copy-start(bf16[1,2,256,256]{3,2,1,0:T(8,128)(2,1)} %param.5) | copy-start | bytes 786436
  33.4 7.9 %copy-start.2 = (s32[4]{0:T(128)S(1)}, s32[4]{0:T(128)}, u32[]{:S(2)}) copy-start(s32[4]{0:T(128)} %param.7) | copy-start | bytes 52
  33.4 85.2 %all-to-all-start = ((bf16[16,4,64,512]{3,2,1,0:T(8,128)(2,1)}), bf16[16,4,64,512]{3,2,1,0:T(8,128)(2,1)}, u32[]{:S(2)}, u32[]{:S(2)}) async-start(bf16[16,4,64,512]{3,2,1,0:T(8,128)(2,1)} %slice_dynamic-update-slice_fusion), calls=%async_computation | async-start | bytes 8388608 | tf_op jit(solution)/shard_map/all_to_all | solution.py:17
  40.9 283.7 %all-reduce.2.cloned.1.call-start = ((), (), s32[]{:S(2)}) async-start(), calls=%async_computation.1 | async-start | bytes 8388608 | tf_op jit(solution)/shard_map/psum | solution.py:29
Sparse Core Ops, SparseCore 0:
  201.7 122.8 all-reduce.1
